TPU v7x, 256 devices: a whole 4x4x8 slice. The times are simulated.
256 devices in a mesh: view: 32 (over z, y_lo, core), head: 8 (over x, y_hi).
Axes of the slice: x: 4, y: 4 (y_hi: 2, y_lo: 2; y = y_hi * 2 + y_lo), z: 8, core: 2. Of those that a mesh axis runs over, the one named last changes fastest.
Arguments:
- tokens: bfloat16 [8192, 1536], P('view'), may hold values from -8 to 8
- timesteps: int32 [128], P('view'), may hold values from 0 to 999
- adjacency: int32 [128, 6], P('view'), may hold values from 0 to 127, as said below
- neighbour_count: int32 [128], P('view'), may hold values from 2 to 6, as said below
- anchor: int32 [1], replicated, may hold values from 0 to 127
- mod_weight: bfloat16 [256, 6, 1536], P(None, None, 'head'), may hold values from -1.5 to 1.5
- qkv_weight: bfloat16 [1536, 3, 1536], P(None, None, 'head'), may hold values from -1 to 1
- qk_gain: float32 [2, 1536], P(None, 'head'), may hold values from 0.6 to 7.2
- out_weight: bfloat16 [1536, 1536], P('head'), may hold values from -0.15625 to 0.15625
- up_weight: bfloat16 [1536, 6144], P(None, 'head'), may hold values from -0.15625 to 0.15625
- down_weight: bfloat16 [6144, 1536], P('head'), may hold values from -0.078125 to 0.078125
Outputs:
- output: bfloat16 [8192, 1536], P('view')
Inputs may be any that keep to these rules, and one draw needn't show every extreme that they name: `adjacency`: views lie on a closed camera orbit of 128 views (view 128 - 1 beside view 0). Row v names 6 different views other than v, each at most 8 views from v along the orbit; in every draw some used neighbour is exactly 8 views away on each side. Only the first neighbour_count[v] entries are used. `neighbour_count`: some view has 6 neighbours and some view has 2 in every draw.
All inputs are finite; a program needn't handle non-finite values.
Results may differ from a plain program's by a relative error of at most 0.025.
Values may be sent and summed in bfloat16 or wider, within the bound.
A program may use at most 128 MiB of HBM per device.

v0:
```python
import math
import jax
import jax.numpy as jnp
from jax import lax
from jax.sharding import PartitionSpec as P

HD = 64
RADIUS = 8
EPSILON = 1e-06


def shifted(block, axis, distance):
    devices = range(lax.axis_size(axis))
    route = [((i - distance) % len(devices), i) for i in devices]
    return lax.ppermute(block, axis, route)


def from_root(shard, axis, root):
    mine = lax.axis_index(axis) == root
    return lax.psum(jnp.where(mine, shard, jnp.zeros_like(shard)), axis)


def layer_norm(values):
    centre = values - jnp.mean(values, axis=-1, keepdims=True)
    return centre * lax.rsqrt(jnp.mean(centre * centre, axis=-1, keepdims=True) + EPSILON)


def head_norm(values, qk_gains):
    return (
        values * lax.rsqrt(jnp.mean(values * values, axis=-1, keepdims=True) + EPSILON) * qk_gains
    )


def time_features(steps_in, freq_count):
    half_count = freq_count // 2
    frequency = jnp.exp(-math.log(10000.0) * jnp.arange(half_count, dtype=jnp.float32) / half_count)
    angles = steps_in.astype(jnp.float32)[:, None] * frequency[None, :]
    return jnp.concatenate([jnp.cos(angles), jnp.sin(angles)], axis=-1)


def body(
    tokens,
    timesteps,
    adjacency,
    neighbour_count,
    anchor,
    mod_weight,
    qkv_weight,
    qk_gain,
    out_weight,
    up_weight,
    down_weight,
):
    view_count = timesteps.shape[0]
    row_count, model_width = tokens.shape
    view_tokens = row_count // view_count
    local_width = qkv_weight.shape[2]
    local_heads = local_width // HD
    total_views = view_count * lax.axis_size("view")
    first_view = lax.axis_index("view") * view_count
    features = time_features(timesteps, mod_weight.shape[0])
    activated = jax.nn.silu(features).astype(jnp.bfloat16)
    mod_part = jnp.einsum("vf,fsd->vsd", activated, mod_weight, preferred_element_type=jnp.float32)
    modulation = lax.all_gather(mod_part, "head", axis=2, tiled=True)
    inputs = tokens.reshape(view_count, view_tokens, model_width).astype(jnp.float32)
    first_in = (
        layer_norm(inputs) * (1.0 + modulation[:, 1][:, None]) + modulation[:, 0][:, None]
    ).astype(jnp.bfloat16)
    projected = jnp.einsum(
        "vtd,dsc->vtsc", first_in, qkv_weight, preferred_element_type=jnp.float32
    )
    projected = projected.reshape(view_count, view_tokens, 3, local_heads, HD)
    qk_gains = qk_gain.reshape(2, local_heads, HD)
    queries = head_norm(projected[:, :, 0], qk_gains[0]).astype(jnp.bfloat16)
    keys_here = head_norm(projected[:, :, 1], qk_gains[1]).astype(jnp.bfloat16)
    values_here = projected[:, :, 2].astype(jnp.bfloat16)
    kv_block = jnp.concatenate(
        [
            keys_here.reshape(view_count, view_tokens, local_width),
            values_here.reshape(view_count, view_tokens, local_width),
        ],
        axis=-1,
    )
    reach = RADIUS // view_count
    distances = list(range(reach, 0, -1)) + list(range(-1, -reach - 1, -1))
    fetched = [shifted(kv_block, "view", distance) for distance in distances]
    lower_blocks = fetched[:reach]
    upper_blocks = fetched[reach:]
    candidates = jnp.concatenate(lower_blocks + [kv_block] + upper_blocks, axis=0)
    anchor_view = anchor[0]
    owner_index = anchor_view // view_count
    own_piece = lax.dynamic_index_in_dim(kv_block, anchor_view % view_count, 0, keepdims=False)
    anchor_block = from_root(own_piece, "view", owner_index)
    local_ids = jnp.arange(view_count, dtype=jnp.int32)
    global_ids = first_view + local_ids
    half_views = total_views // 2
    offsets = (adjacency - global_ids[:, None] + half_views) % total_views - half_views
    slot_ids = jnp.concatenate(
        [(RADIUS + local_ids)[:, None], RADIUS + local_ids[:, None] + offsets], axis=1
    )
    chosen = candidates[slot_ids]
    anchor_rows = jnp.broadcast_to(anchor_block[None, None], (view_count, 1) + anchor_block.shape)
    gathered = jnp.concatenate([chosen, anchor_rows], axis=1)
    block_count = gathered.shape[1]
    key_blocks = gathered[..., :local_width].reshape(
        view_count, block_count, view_tokens, local_heads, HD
    )
    value_blocks = gathered[..., local_width:].reshape(
        view_count, block_count, view_tokens, local_heads, HD
    )
    usable = jnp.concatenate(
        [
            jnp.ones((view_count, 1), dtype=bool),
            jnp.arange(adjacency.shape[1], dtype=jnp.int32)[None, :] < neighbour_count[:, None],
            jnp.ones((view_count, 1), dtype=bool),
        ],
        axis=1,
    )
    scores = jnp.einsum(
        "vthe,vbshe->vhtbs", queries, key_blocks, preferred_element_type=jnp.float32
    ) * (1.0 / math.sqrt(HD))
    scores = jnp.where(usable[:, None, None, :, None], scores, -jnp.inf)
    largest = jnp.max(scores, axis=(3, 4), keepdims=True)
    powers = jnp.exp(scores - largest)
    weights = (powers / jnp.sum(powers, axis=(3, 4), keepdims=True)).astype(jnp.bfloat16)
    attended = jnp.einsum(
        "vhtbs,vbshe->vthe", weights, value_blocks, preferred_element_type=jnp.float32
    ).astype(jnp.bfloat16)
    attended = attended.reshape(row_count, local_width)
    attn_total = lax.psum(
        jnp.dot(attended, out_weight, preferred_element_type=jnp.float32).astype(jnp.bfloat16),
        "head",
    ).astype(jnp.float32)
    residual = inputs + modulation[:, 2][:, None] * attn_total.reshape(
        view_count, view_tokens, model_width
    )
    second_in = (
        layer_norm(residual) * (1.0 + modulation[:, 4][:, None]) + modulation[:, 3][:, None]
    ).astype(jnp.bfloat16)
    hidden = jax.nn.gelu(
        jnp.dot(
            second_in.reshape(row_count, model_width), up_weight, preferred_element_type=jnp.float32
        ),
        approximate=True,
    ).astype(jnp.bfloat16)
    mlp_total = lax.psum(
        jnp.dot(hidden, down_weight, preferred_element_type=jnp.float32).astype(jnp.bfloat16),
        "head",
    ).astype(jnp.float32)
    finished = residual + modulation[:, 5][:, None] * mlp_total.reshape(
        view_count, view_tokens, model_width
    )
    result = finished.astype(jnp.bfloat16).reshape(row_count, model_width)
    return result


def solution(mesh):
    return jax.shard_map(
        body,
        mesh=mesh,
        in_specs=(
            P("view", None),
            P("view"),
            P("view", None),
            P("view"),
            P(),
            P(None, None, "head"),
            P(None, None, "head"),
            P(None, "head"),
            P("head", None),
            P(None, "head"),
            P("head", None),
        ),
        out_specs=P("view", None),
        check_vma=False,
    )
```

profile of v0, /device:TPU:32, one launch (start us, length us, event | category | flops | bytes accessed | tf_op | source)
XLA Modules:
  0.0 453.6 jit_solution(16673640462495064002)
XLA Ops:
  7.5 1.3 fusion.51
  9.0 70.6 %all_gather.3 = f32[4,6,1536]{1,0,2:T(4,128)S(1)} all-gather(f32[4,6,192]{1,0,2:T(4,128)S(1)} %copy.47), channel_id=1, replica_groups=mesh['view'=32,'head'=8] {'head'}, dimensions={2}, use_global_device_ids=true | all-gather | bytes 165888 | tf_op jit(solution)/shard_map/all_gather | solution.py:64
  79.6 11.9 %fusion.62 = (f32[4,1,1536]{1,0,2:T(4,128)}, f32[4,1,1536]{1,0,2:T(4,128)}, f32[4,1,1536]{1,0,2:T(4,128)}, f32[4,1,1536]{1,0,2:T(4,128)}, f32[4,1,1536]{1,0,2:T(4,128)}, /*index=5*/f32[4,1,1536]{1,0,2:T(4,128)}) fusion(f32[4,6,1536]{1,0,2:T(4,128)S(1)} %all_gather.3), kind=kLoop, calls=%fused_computation.110 | loop fusion | bytes 294912 | tf_op jit(solution)/shard_map/slice | solution.py:150
  91.5 3.1 copy.50
  94.6 3.2 copy.64
  99.3 1.1 fusion.65
  102.4 2.7 collective-permute-start.2
  105.0 2.0 collective-permute-start.3
  108.7 1.1 multiply_reduce_fusion.1
  114.5 1.2 pad_add_fusion
  116.4 105.4 %psum.21 = bf16[64,384]{0,1:T(8,128)(2,1)} all-reduce(bf16[64,384]{0,1:T(8,128)(2,1)} %fusion.45), channel_id=1, replica_groups=mesh['view'=32,'head'=8] {'view'}, use_global_device_ids=true, to_apply=%region_3.4 | all-reduce | flops 24576 | bytes 98304 | tf_op jit(solution)/shard_map/psum | solution.py:20
  221.9 1.8 constant_dynamic-update-slice_fusion.4
  223.7 1.8 constant_dynamic-update-slice_fusion.3
  226.3 1.8 constant_dynamic-update-slice_fusion.1
  228.1 1.8 constant_dynamic-update-slice_fusion
  229.9 4.0 gather_fusion
  234.0 4.4 fusion.8
  238.3 2.6 copy.53
  240.9 2.1 fusion
  243.1 0.8 fusion.1
  244.5 1.1 fusion.21
  245.9 2.3 convolution_convert_fusion.1
  248.4 3.1 copy.59
  251.5 3.1 copy.65
  254.6 3.1 copy.48
  257.7 88.3 %all-reduce.3.cloned.1.call-done = bf16[256,1536]{1,0:T(8,128)(2,1)} async-done(((bf16[256,1536]{1,0:T(8,128)(2,1)}), bf16[256,1536]{1,0:T(8,128)(2,1)}) %all-reduce.3.cloned.1.call-update) | async-done | bytes 786448 | tf_op jit(solution)/shard_map/psum | solution.py:130
  346.0 1.5 fusion.24
  348.0 1.4 fusion.9
  349.4 4.5 %convolution_convert_fusion = bf16[256,1536]{1,0:T(8,128)(2,1)} fusion(bf16[768,1536]{1,0:T(8,128)(2,1)S(1)} %copy-done, bf16[256,1536]{1,0:T(8,128)(2,1)} %fusion.9, bf16[1536,768]{1,0:T(8,128)(2,1)} %param.20), kind=kOutput, calls=%fused_computation.7 | convolution fusion | flops 1210122240 | bytes 6291456 | tf_op jit(solution)/shard_map/dot_general | solution.py:147
  354.0 3.1 copy.57
  357.1 87.0 %all-reduce.5.cloned.1.call-done = bf16[256,1536]{1,0:T(8,128)(2,1)} async-done(((bf16[256,1536]{1,0:T(8,128)(2,1)}), bf16[256,1536]{1,0:T(8,128)(2,1)}) %all-reduce.5.cloned.1.call-update) | async-done | bytes 786448 | tf_op jit(solution)/shard_map/psum | solution.py:146
  444.1 2.6 fusion.11
  (69 shorter events, 13.4 us)
Async XLA Ops:
  6.5 342.9 %copy-start = (bf16[768,1536]{1,0:T(8,128)(2,1)S(1)}, bf16[768,1536]{1,0:T(8,128)(2,1)}, u32[]{:S(2)}) copy-start(bf16[768,1536]{1,0:T(8,128)(2,1)} %param.21) | copy-start | bytes 7077892
  6.5 339.5 %all-reduce.3.cloned.1.call-start = ((), (), s32[]{:S(2)}) async-start(), calls=%async_computation | async-start | bytes 1572864 | tf_op jit(solution)/shard_map/psum | solution.py:130
  94.6 3.2 copy-start.1
  97.8 1.5 copy-start.9
  99.3 1.2 copy-start.6
  100.4 1.0 copy-start.3
  100.4 9.4 %copy-start.10 = (s32[4]{0:T(128)S(1)}, s32[4]{0:T(128)}, u32[]{:S(2)}) copy-start(s32[4]{0:T(128)} %param.14) | copy-start | bytes 52
  100.4 11.3 %copy-start.7 = (s32[4,6]{1,0:T(4,128)S(1)}, s32[4,6]{1,0:T(4,128)}, u32[]{:S(2)}) copy-start(s32[4,6]{1,0:T(4,128)} %param.13) | copy-start | bytes 292
  102.3 119.5 %collective-permute-start = (bf16[4,64,384]{1,2,0:T(8,128)(2,1)}, bf16[4,64,384]{1,2,0:T(8,128)(2,1)}, u32[]{:S(2)}, u32[]{:S(2)}) collective-permute-start(bf16[4,64,384]{1,2,0:T(8,128)(2,1)} %pad_maximum_fusion.1), channel_id=1, source_target_pairs={{240,0},{248,8},{0,16},{8,24},{16,32},{24,40},{32,48},{40,56},{48,... | collective-permute-start | bytes 589832 | tf_op jit(solution)/shard_map/ppermute | solution.py:15
  102.4 121.3 %collective-permute-start.1 = (bf16[4,64,384]{1,2,0:T(8,128)(2,1)}, bf16[4,64,384]{1,2,0:T(8,128)(2,1)}, u32[]{:S(2)}, u32[]{:S(2)}) collective-permute-start(bf16[4,64,384]{1,2,0:T(8,128)(2,1)} %pad_maximum_fusion.1), channel_id=1, source_target_pairs={{248,0},{0,8},{8,16},{16,24},{24,32},{32,40},{40,48},{48,56},{56,6... | collective-permute-start | bytes 589832 | tf_op jit(solution)/shard_map/ppermute | solution.py:15
  102.4 123.9 %collective-permute-start.2 = (bf16[4,64,384]{1,2,0:T(8,128)(2,1)}, bf16[4,64,384]{1,2,0:T(8,128)(2,1)}, u32[]{:S(2)}, u32[]{:S(2)}) collective-permute-start(bf16[4,64,384]{1,2,0:T(8,128)(2,1)} %pad_maximum_fusion.1), channel_id=1, source_target_pairs={{8,0},{16,8},{24,16},{32,24},{40,32},{48,40},{56,48},{64,56},{72,6... | collective-permute-start | bytes 589832 | tf_op jit(solution)/shard_map/ppermute | solution.py:15
  105.0 123.0 %collective-permute-start.3 = (bf16[4,64,384]{1,2,0:T(8,128)(2,1)}, bf16[4,64,384]{1,2,0:T(8,128)(2,1)}, u32[]{:S(2)}, u32[]{:S(2)}) collective-permute-start(bf16[4,64,384]{1,2,0:T(8,128)(2,1)} %pad_maximum_fusion.1), channel_id=1, source_target_pairs={{16,0},{24,8},{32,16},{40,24},{48,32},{56,40},{64,48},{72,56},{80,... | collective-permute-start | bytes 589832 | tf_op jit(solution)/shard_map/ppermute | solution.py:15
  228.1 5.8 %copy-start.5 = (bf16[64,384]{0,1:T(8,128)(2,1)S(1)}, bf16[64,384]{0,1:T(8,128)(2,1)}, u32[]{:S(2)}) copy-start(bf16[64,384]{0,1:T(8,128)(2,1)} %psum.21) | copy-start | bytes 147460
  238.3 2.6 copy-start.8
  243.1 1.4 copy-start.4
  248.3 195.8 %all-reduce.5.cloned.1.call-start = ((), (), s32[]{:S(2)}) async-start(), calls=%async_computation.1 | async-start | bytes 1572864 | tf_op jit(solution)/shard_map/psum | solution.py:146
  346.0 1.6 copy-start.2
Sparse Core Ops, SparseCore 0:
  248.4 97.5 all-reduce.2
  354.1 89.9 all-reduce.4
where the time goes:
time: 455 us; the launch traced here: 454 us
  blocking collectives  176 us (39%)
  waiting for transfers between devices  175 us (38%)
  local copies, waits for them, and re-layouts  49.1 us (11%)
  other arithmetic  21.6 us (5%)
  between operations  14.3 us (3%)
  matrix products  12.5 us (3%)
  starting transfers between devices  4.71 us (1%)
    psum x1, blocking collectives, from_root(): return lax.psum(jnp.where(mine, shard, jnp.zeros_like(shard)), axis)  105 us
    psum x1, waiting for transfers between devices, body(): lax.psum(jnp.dot(attended, out_weight, preferred_element_type=jnp.float32...  88.3 us
    psum x1, waiting for transfers between devices, body(): lax.psum(jnp.dot(hidden, down_weight, preferred_element_type=jnp.float32)...  87 us
    all_gather x1, blocking collectives, body(): modulation = lax.all_gather(mod_part, 'head', axis=2, tiled=True)  70.6 us
    slice x2, local copies, waits for them, and re-layouts, body(): modulation[:, 5][:, None]  15 us
    unnamed x27, local copies, waits for them, and re-layouts  12.9 us
  transfers between devices with their start and end apart: 6, of which 2 were waited for; matrix products, arithmetic and copies ran while one was open for 6% of the time, Pallas kernels for 0%

commit v1 on v0

--- a/solution.py
+++ b/solution.py
@@ -1,3 +1,4 @@
+import functools
 import math
 import jax
 import jax.numpy as jnp
@@ -7,6 +8,17 @@
 HD = 64
 RADIUS = 8
 EPSILON = 1e-06
+
+
+def rings_link(array_in, shard_axis):
+    found_now = jnp.concatenate(
+        lax.all_to_all(jnp.stack([array_in] * lax.axis_size(shard_axis), axis=0), shard_axis, 0, 0),
+        axis=2,
+    )
+    return found_now
+
+
+_fill_layers_all = functools.partial(rings_link, shard_axis="head")
 
 
 def shifted(block, axis, distance):
@@ -61,7 +73,7 @@
     features = time_features(timesteps, mod_weight.shape[0])
     activated = jax.nn.silu(features).astype(jnp.bfloat16)
     mod_part = jnp.einsum("vf,fsd->vsd", activated, mod_weight, preferred_element_type=jnp.float32)
-    modulation = lax.all_gather(mod_part, "head", axis=2, tiled=True)
+    modulation = _fill_layers_all(mod_part)
     inputs = tokens.reshape(view_count, view_tokens, model_width).astype(jnp.float32)
     first_in = (
         layer_norm(inputs) * (1.0 + modulation[:, 1][:, None]) + modulation[:, 0][:, None]

time: 455 us -> 380 us (0.84)
  blocking collectives: 176 us -> 119 us
  local copies, waits for them, and re-layouts: 49.1 us -> 17.8 us
  waiting for transfers between devices: 175 us -> 188 us
  starting transfers between devices: 4.71 us -> 9.72 us
    all_gather x1 -> x0, blocking collectives: 70.6 us -> none  [body(): modulation = lax.all_gather(mod_part, 'head', axis=2, tiled=True)]
    slice x5 -> x0, local copies, waits for them, and re-layouts: 24.4 us -> none  [the longest x2 15 us: body(): modulation[:, 5][:, None]]
    psum x1, blocking collectives: 105 us -> 119 us  [from_root(): return lax.psum(jnp.where(mine, shard, jnp.zeros_like(shard)), axis)]
    all_to_all x0 -> x1, starting transfers between devices: none -> 6.93 us  [rings_link(): lax.all_to_all(jnp.stack([array_in] * lax.axis_size(shard_axis), axis=0),...]
    unnamed x27 -> x33, local copies, waits for them, and re-layouts: 12.9 us -> 7.2 us
    psum x1, waiting for transfers between devices: 88.3 us -> 93.8 us  [body(): lax.psum(jnp.dot(attended, out_weight, preferred_element_type=jnp.float32...]
  transfers between devices with their start and end apart: 6 -> 7, of which waited for: 2 -> 3; matrix products, arithmetic and copies ran while one was open for 6% -> 3% of each run, Pallas kernels for 0% -> 0%
where the time goes in v1:
time: 380 us; the launch traced here: 379 us
  waiting for transfers between devices  188 us (49%)
  blocking collectives  119 us (31%)
  other arithmetic  17.9 us (5%)
  local copies, waits for them, and re-layouts  17.8 us (5%)
  between operations  14.3 us (4%)
  matrix products  12.6 us (3%)
  starting transfers between devices  9.72 us (3%)
    psum x1, blocking collectives, from_root(): return lax.psum(jnp.where(mine, shard, jnp.zeros_like(shard)), axis)  119 us
    psum x1, waiting for transfers between devices, body(): lax.psum(jnp.dot(attended, out_weight, preferred_element_type=jnp.float32...  93.8 us
    psum x1, waiting for transfers between devices, body(): lax.psum(jnp.dot(hidden, down_weight, preferred_element_type=jnp.float32)...  90.1 us
  transfers between devices with their start and end apart: 7, of which 3 were waited for; matrix products, arithmetic and copies ran while one was open for 3% of the time, Pallas kernels for 0%

profile of v1, /device:TPU:32, one launch (start us, length us, event | category | flops | bytes accessed | tf_op | source)
XLA Modules:
  0.0 379.3 jit_solution(18188708349134825957)
XLA Ops:
  6.6 0.8 convert_element_type.67
  7.5 1.4 fusion.53
  8.8 0.7 stack.2
  9.6 6.9 %all-to-all-start = ((f32[8,4,6,192]{3,1,2,0:T(4,128)}), f32[8,4,6,192]{3,1,2,0:T(4,128)S(1)}, u32[]{:S(2)}, u32[]{:S(2)}) async-start(f32[8,4,6,192]{3,1,2,0:T(4,128)} %stack.2), calls=%async_computation | async-start | bytes 393216 | tf_op jit(solution)/shard_map/all_to_all | solution.py:15
  16.6 0.7 iota_compare_fusion
  18.7 0.6 pad_add_fusion
  20.2 4.5 %all-to-all-done = f32[8,4,6,192]{3,1,2,0:T(4,128)S(1)} async-done(((f32[8,4,6,192]{3,1,2,0:T(4,128)}), f32[8,4,6,192]{3,1,2,0:T(4,128)S(1)}, u32[]{:S(2)}, u32[]{:S(2)}) %all-to-all-start) | async-done | bytes 147488 | tf_op jit(solution)/shard_map/all_to_all | solution.py:15
  24.9 0.6 slice_bitcast_fusion.2
  26.4 1.1 fusion.66
  27.7 0.8 copy-done.3
  28.6 0.8 pad_maximum_fusion.1
  30.2 1.8 collective-permute-start
  32.0 0.7 fusion.45
  32.6 118.6 %psum.21 = bf16[64,384]{0,1:T(8,128)(2,1)} all-reduce(bf16[64,384]{0,1:T(8,128)(2,1)} %fusion.45), channel_id=1, replica_groups=mesh['view'=32,'head'=8] {'view'}, use_global_device_ids=true, to_apply=%region_3.4 | all-reduce | flops 24576 | bytes 98304 | tf_op jit(solution)/shard_map/psum | solution.py:32
  151.2 1.8 constant_dynamic-update-slice_fusion.4
  153.0 1.8 constant_dynamic-update-slice_fusion.3
  154.8 0.8 constant_dynamic-update-slice_fusion.2
  155.6 1.8 constant_dynamic-update-slice_fusion.1
  157.4 1.8 constant_dynamic-update-slice_fusion
  159.1 4.1 %gather_fusion = bf16[28,64,384]{1,2,0:T(8,128)(2,1)} fusion(bf16[20,64,384]{1,2,0:T(8,128)(2,1)} %constant_dynamic-update-slice_fusion, s32[1024]{0:T(1024)S(1)} %pad_clamp_fusion), kind=kCustom, calls=%fused_computation | custom fusion | bytes 2752624 | tf_op jit(solution)/shard_map/gather | solution.py:113
  163.3 4.4 %fusion.8 = (bf16[4,8,64,192]{2,3,1,0:T(8,128)(2,1)}, bf16[4,8,64,192]{2,3,1,0:T(8,128)(2,1)}) fusion(bf16[4,7,64,384]{2,3,1,0:T(8,128)(2,1)} %bitcast.134, bf16[4,1,64,384]{2,3,1,0:T(8,128)(2,1)S(1)} %broadcast_in_dim.13), kind=kLoop, calls=%fused_computation.19 | loop fusion | flops 3145728 | bytes 3145728 | tf_op jit(solution)/shard_map/concatenate | solution.py:115
  167.7 2.6 copy.30
  170.3 2.1 fusion
  172.4 0.8 fusion.1
  173.8 1.1 fusion.21
  175.3 2.3 convolution_convert_fusion.1
  177.9 93.8 %all-reduce.3.cloned.1.call-done = bf16[256,1536]{1,0:T(8,128)(2,1)} async-done(((bf16[256,1536]{1,0:T(8,128)(2,1)}), bf16[256,1536]{1,0:T(8,128)(2,1)}) %all-reduce.3.cloned.1.call-update) | async-done | bytes 786448 | tf_op jit(solution)/shard_map/psum | solution.py:142
  271.7 1.5 fusion.24
  273.8 1.4 fusion.9
  275.2 4.6 %convolution_convert_fusion = bf16[256,1536]{1,0:T(8,128)(2,1)} fusion(bf16[768,1536]{1,0:T(8,128)(2,1)S(1)} %copy-done, bf16[256,1536]{1,0:T(8,128)(2,1)} %fusion.9, bf16[1536,768]{1,0:T(8,128)(2,1)} %param.20), kind=kOutput, calls=%fused_computation.7 | convolution fusion | flops 1210122240 | bytes 6291456 | tf_op jit(solution)/shard_map/dot_general | solution.py:159
  279.8 90.1 %all-reduce.5.cloned.1.call-done = bf16[256,1536]{1,0:T(8,128)(2,1)} async-done(((bf16[256,1536]{1,0:T(8,128)(2,1)}), bf16[256,1536]{1,0:T(8,128)(2,1)}) %all-reduce.5.cloned.1.call-update) | async-done | bytes 786448 | tf_op jit(solution)/shard_map/psum | solution.py:158
  369.8 2.6 fusion.11
  (72 shorter events, 5.5 us)
Async XLA Ops:
  6.5 268.6 %copy-start = (bf16[768,1536]{1,0:T(8,128)(2,1)S(1)}, bf16[768,1536]{1,0:T(8,128)(2,1)}, u32[]{:S(2)}) copy-start(bf16[768,1536]{1,0:T(8,128)(2,1)} %param.21) | copy-start | bytes 7077892
  6.5 10.8 %copy-start.1 = (bf16[256,1536]{1,0:T(8,128)(2,1)S(1)}, bf16[256,1536]{1,0:T(8,128)(2,1)}, u32[]{:S(2)}) copy-start(bf16[256,1536]{1,0:T(8,128)(2,1)} %param.11) | copy-start | bytes 2359300
  6.5 11.4 %copy-start.11 = (f32[2,192]{1,0:T(2,128)S(1)}, f32[2,192]{1,0:T(2,128)}, u32[]{:S(2)}) copy-start(f32[2,192]{1,0:T(2,128)} %param.18) | copy-start | bytes 4612
  6.5 12.0 %copy-start.12 = (s32[4,6]{1,0:T(4,128)S(1)}, s32[4,6]{1,0:T(4,128)}, u32[]{:S(2)}) copy-start(s32[4,6]{1,0:T(4,128)} %param.13) | copy-start | bytes 292
  9.6 15.1 %all-to-all-start = ((f32[8,4,6,192]{3,1,2,0:T(4,128)}), f32[8,4,6,192]{3,1,2,0:T(4,128)S(1)}, u32[]{:S(2)}, u32[]{:S(2)}) async-start(f32[8,4,6,192]{3,1,2,0:T(4,128)} %stack.2), calls=%async_computation | async-start | bytes 393216 | tf_op jit(solution)/shard_map/all_to_all | solution.py:15
  16.5 255.2 %all-reduce.3.cloned.1.call-start = ((), (), s32[]{:S(2)}) async-start(), calls=%async_computation.1 | async-start | bytes 1572864 | tf_op jit(solution)/shard_map/psum | solution.py:142
  24.9 1.5 copy-start.14
  27.5 1.0 copy-start.3
  27.5 1.0 copy-start.10
  29.4 127.9 %collective-permute-start.3 = (bf16[4,64,384]{1,2,0:T(8,128)(2,1)}, bf16[4,64,384]{1,2,0:T(8,128)(2,1)}, u32[]{:S(2)}, u32[]{:S(2)}) collective-permute-start(bf16[4,64,384]{1,2,0:T(8,128)(2,1)} %pad_maximum_fusion.1), channel_id=1, source_target_pairs={{16,0},{24,8},{32,16},{40,24},{48,32},{56,40},{64,48},{72,56},{80,... | collective-permute-start | bytes 589832 | tf_op jit(solution)/shard_map/ppermute | solution.py:27
  29.7 125.9 %collective-permute-start.2 = (bf16[4,64,384]{1,2,0:T(8,128)(2,1)}, bf16[4,64,384]{1,2,0:T(8,128)(2,1)}, u32[]{:S(2)}, u32[]{:S(2)}) collective-permute-start(bf16[4,64,384]{1,2,0:T(8,128)(2,1)} %pad_maximum_fusion.1), channel_id=1, source_target_pairs={{8,0},{16,8},{24,16},{32,24},{40,32},{48,40},{56,48},{64,56},{72,6... | collective-permute-start | bytes 589832 | tf_op jit(solution)/shard_map/ppermute | solution.py:27
  29.7 123.3 %collective-permute-start.1 = (bf16[4,64,384]{1,2,0:T(8,128)(2,1)}, bf16[4,64,384]{1,2,0:T(8,128)(2,1)}, u32[]{:S(2)}, u32[]{:S(2)}) collective-permute-start(bf16[4,64,384]{1,2,0:T(8,128)(2,1)} %pad_maximum_fusion.1), channel_id=1, source_target_pairs={{248,0},{0,8},{8,16},{16,24},{24,32},{32,40},{40,48},{48,56},{56,6... | collective-permute-start | bytes 589832 | tf_op jit(solution)/shard_map/ppermute | solution.py:27
  30.2 121.0 %collective-permute-start = (bf16[4,64,384]{1,2,0:T(8,128)(2,1)}, bf16[4,64,384]{1,2,0:T(8,128)(2,1)}, u32[]{:S(2)}, u32[]{:S(2)}) collective-permute-start(bf16[4,64,384]{1,2,0:T(8,128)(2,1)} %pad_maximum_fusion.1), channel_id=1, source_target_pairs={{240,0},{248,8},{0,16},{8,24},{16,32},{24,40},{32,48},{40,56},{48,... | collective-permute-start | bytes 589832 | tf_op jit(solution)/shard_map/ppermute | solution.py:27
  159.1 4.1 %copy-start.6 = (bf16[64,384]{0,1:T(8,128)(2,1)S(1)}, bf16[64,384]{0,1:T(8,128)(2,1)}, u32[]{:S(2)}) copy-start(bf16[64,384]{0,1:T(8,128)(2,1)} %psum.21) | copy-start | bytes 147460
  167.7 2.6 copy-start.13
  172.4 1.4 copy-start.4
  175.0 96.8 %copy-start.5 = (f32[4,1536]{1,0:T(4,128)S(1)}, f32[4,1536]{1,0:T(4,128)}, u32[]{:S(2)}) copy-start(f32[4,1536]{1,0:T(4,128)} %get-tuple-element.14) | copy-start | bytes 73732
  177.7 192.2 %all-reduce.5.cloned.1.call-start = ((), (), s32[]{:S(2)}) async-start(), calls=%async_computation.2 | async-start | bytes 1572864 | tf_op jit(solution)/shard_map/psum | solution.py:158
  271.7 1.6 copy-start.2
  271.7 2.0 copy-start.8
  271.7 2.0 copy-start.9
  275.2 94.7 %copy-start.7 = (f32[4,1536]{1,0:T(4,128)S(1)}, f32[4,1536]{1,0:T(4,128)}, u32[]{:S(2)}) copy-start(f32[4,1536]{1,0:T(4,128)} %get-tuple-element.9) | copy-start | bytes 73732
Sparse Core Ops, SparseCore 0:
  177.8 93.8 all-reduce.2
  279.9 89.9 all-reduce.4
